TPU v7x, 128 devices: a whole 4x4x4 slice. The times are simulated.
128 devices in a mesh: row: 8 (over z, core), col: 16 (over y, x).
Axes of the slice: x: 4, y: 4, z: 4, core: 2. Of those that a mesh axis runs over, the one named last changes fastest.
Arguments:
- panel_blocks: bfloat16 [16, 8, 512, 512], P('col', None, 'row'), may hold values from -0.25 to 0.25
- factor_inverse: bfloat16 [16, 512, 512], P('col')
- target_rows: int32 [16, 8], replicated, may hold values from 0 to 15, as said below
- owner_order: int32 [16], replicated, may hold values from 0 to 15, each once
- ancestor_rows: float32 [16, 512, 8192], P('col', 'row'), may hold values from -1.8 to 1.8
Outputs:
- updated_rows: float32 [16, 512, 8192], P('col', 'row')
Inputs may be any that keep to these rules, and one draw needn't show every extreme that they name: `target_rows`: each row names 8 different ancestor block rows in ascending order; each index of col holds exactly one supernode. `owner_order`: each ancestor block row once.
All inputs are finite; a program needn't handle non-finite values.
Results may differ from a plain program's by a relative error of at most 0.0024.
Values may be sent and summed in bfloat16 or wider, within the bound.
A program may use at most 192 MiB of HBM per device.

v0:
```python
import jax
import jax.numpy as jnp
from jax import lax
from jax.sharding import PartitionSpec as P


def solve_rows(blocks, factor_inverse):
    return jnp.einsum(
        "spiw,svw->spiv", blocks, factor_inverse, preferred_element_type=jnp.float32
    ).astype(jnp.bfloat16)


def pick_rows(products, own_targets, order_part):
    matched = own_targets[None, :, :] == order_part[:, None, None]
    places = lax.broadcasted_iota(jnp.int32, matched.shape, 2)
    position = jnp.sum(jnp.where(matched, places, 0), axis=2)
    present = jnp.any(matched, axis=2)
    supernode_ids = lax.broadcasted_iota(jnp.int32, position.shape, 1)
    chosen = products[supernode_ids, position]
    return jnp.where(present[:, :, None, None, None], chosen, jnp.zeros((), chosen.dtype))


def body(panel_blocks, factor_inverse, target_rows, owner_order, ancestor_rows):
    supernodes = panel_blocks.shape[0]
    own_height = panel_blocks.shape[2]
    width = panel_blocks.shape[3]
    ancestors = owner_order.shape[0]
    col_place = lax.axis_index("col")
    own_targets = lax.dynamic_slice_in_dim(target_rows, col_place * supernodes, supernodes, 0)
    own_solved = solve_rows(panel_blocks, factor_inverse)
    products = jnp.einsum(
        "spiw,sqmw->spiqm",
        own_solved,
        lax.all_gather(own_solved, "row", axis=2, tiled=True),
        preferred_element_type=jnp.float32,
    ).astype(jnp.bfloat16)
    block_ids = lax.broadcasted_iota(jnp.int32, (1, 1, 1, ancestors), 3)
    own_onehot = (own_targets[:, :, None] == block_ids[0]).astype(jnp.bfloat16)
    chosen = pick_rows(products, own_targets, owner_order)
    spread = jnp.einsum("sqb,jsiqw->jibw", own_onehot, chosen, preferred_element_type=jnp.float32)
    summed = lax.psum_scatter(
        spread.reshape(
            ancestor_rows.shape[0] * lax.axis_size("col"), own_height, ancestors * width
        ),
        "col",
        scatter_dimension=0,
        tiled=True,
    )
    return ancestor_rows - summed


def solution(mesh):
    return jax.shard_map(
        body,
        mesh=mesh,
        in_specs=(
            P("col", None, "row", None),
            P("col", None, None),
            P(),
            P(),
            P("col", "row", None),
        ),
        out_specs=P("col", "row", None),
        check_vma=False,
    )
```

profile of v0, /device:TPU:1, one launch (start us, length us, event | category | flops | bytes accessed | tf_op | source)
XLA Modules:
  0.0 327.6 jit_solution(10191502747342464816)
XLA Ops:
  6.5 0.0 copy-start
  6.5 0.0 all-gather.3.cloned.1.call-start
  6.5 1.0 copy-done
  7.6 2.3 convolution_convert_fusion
  9.9 0.0 all-gather.3.cloned.1.call-update
  9.9 0.0 reduce-scatter.4.cloned.1.call-start
  10.0 0.9 dynamic-slice_reduce_fusion
  10.8 0.7 fusion.9
  11.6 0.7 compare_reduce_fusion
  12.3 33.7 %all-gather.3.cloned.1.call-done = bf16[8,512,512]{2,1,0:T(8,128)(2,1)} async-done(((bf16[8,64,512]{2,1,0:T(8,128)(2,1)}), bf16[8,512,512]{2,1,0:T(8,128)(2,1)}) %all-gather.3.cloned.1.call-update) | async-done | bytes 4194320 | tf_op jit(solution)/shard_map/all_gather | solution.py:34
  46.1 6.7 %convert_bitcast_fusion = bf16[1,8,64,8,512]{4,2,3,1,0:T(8,128)(2,1)} fusion(bf16[8,512,512]{2,1,0:T(8,128)(2,1)} %all-gather.3.cloned.1.call-done, bf16[8,64,512]{2,1,0:T(8,128)(2,1)} %convolution_convert_fusion), kind=kOutput, calls=%fused_computation.7 | convolution fusion | flops 2149580800 | bytes 8912896 | tf_op jit(solution)/shard_map/spiw,sqmw->spiqm/dot_general | solution.py:31
  52.7 6.9 %gather_fusion = bf16[16,64,8,512]{3,1,2,0:T(8,128)(2,1)} fusion(bf16[1,8,64,8,512]{4,2,3,1,0:T(8,128)(2,1)} %convert_bitcast_fusion, s32[16]{0:T(128)S(1)} %or_bitcast_fusion), kind=kCustom, calls=%fused_computation | custom fusion | bytes 16777344 | tf_op jit(solution)/shard_map/gather | solution.py:19
  59.6 7.2 %fusion = bf16[16,64,8,512]{3,1,2,0:T(8,128)(2,1)} fusion(bf16[16,64,8,512]{3,1,2,0:T(8,128)(2,1)} %gather_fusion, pred[16]{0:T(512)(128)(4,1)S(1)} %compare_reduce_fusion), kind=kLoop, calls=%fused_computation.3 | loop fusion | flops 4194304 | bytes 16777232 | tf_op jit(solution)/shard_map/jit(_where)/select_n | solution.py:20
  66.8 20.6 %convolution_bitcast_fusion = f32[16,64,16,512]{3,2,1,0:T(8,128)} fusion(bf16[16,64,8,512]{3,1,2,0:T(8,128)(2,1)} %fusion, s32[8]{0:T(128)S(1)} %dynamic-slice_reduce_fusion), kind=kOutput, calls=%fused_computation.1 | convolution fusion | flops 134217856 | bytes 41943072 | tf_op jit(solution)/shard_map/sqb,jsiqw->jibw/dot_general | solution.py:40
  87.4 35.9 %reshape.219 = f32[16,64,8192]{2,1,0:T(8,128)} reshape(f32[16,64,16,512]{3,2,1,0:T(8,128)} %convolution_bitcast_fusion) | data formatting | bytes 67108864 | tf_op jit(solution)/shard_map/reshape | solution.py:42
  123.3 0.0 copy-start.2
  123.3 0.0 reduce-scatter.4.cloned.1.call-update
  123.3 0.0 copy-start.1
  123.3 194.3 %reduce-scatter.4.cloned.1.call-done = f32[1,64,8192]{2,1,0:T(8,128)} async-done(((f32[16,64,8192]{2,1,0:T(8,128)}), f32[1,64,8192]{2,1,0:T(8,128)}) %reduce-scatter.4.cloned.1.call-update) | async-done | bytes 2097168
  317.6 0.0 copy-done.2
  317.6 3.1 sub.3
  320.7 0.0 copy-done.1
  (3 shorter events, 0.0 us)
Async XLA Ops:
  6.5 1.0 copy-start
  6.5 39.5 %all-gather.3.cloned.1.call-start = ((), (), s32[]{:S(2)}) async-start(), calls=%async_computation.1 | async-start | bytes 4718592 | tf_op jit(solution)/shard_map/all_gather | solution.py:34
  9.9 307.7 %reduce-scatter.4.cloned.1.call-start = ((), (), s32[]{:S(2)}) async-start(), calls=%async_computation.2 | async-start | bytes 35651584
  123.3 194.3 %copy-start.2 = (f32[1,64,8192]{2,1,0:T(8,128)S(1)}, f32[1,64,8192]{2,1,0:T(8,128)}, u32[]{:S(2)}) copy-start(f32[1,64,8192]{2,1,0:T(8,128)} %param.9) | copy-start | bytes 6291460
  123.3 197.4 %copy-start.1 = (bf16[1,512,512]{2,1,0:T(8,128)(2,1)S(1)}, bf16[1,512,512]{2,1,0:T(8,128)(2,1)}, u32[]{:S(2)}) copy-start(bf16[1,512,512]{2,1,0:T(8,128)(2,1)} %param.6) | copy-start | bytes 1572868
Sparse Core Ops, SparseCore 0:
  10.0 35.9 all-gather.2
  123.4 194.1 reduce-scatter.3
where the time goes:
time: 329 us; the launch traced here: 328 us
  waiting for transfers between devices  228 us (69%)
  local copies, waits for them, and re-layouts  44.7 us (14%)
  matrix products  29.6 us (9%)
  between operations  13.4 us (4%)
  other arithmetic  11.8 us (4%)
    unnamed x3, waiting for transfers between devices  194 us
    reshape x1, local copies, waits for them, and re-layouts, body(): spread.reshape(ancestor_rows.shape[0] * lax.axis_size('col'), own_height,...  35.9 us
    all_gather x1, waiting for transfers between devices, body(): lax.all_gather(own_solved, 'row', axis=2, tiled=True)  33.7 us
    dot_general x1, matrix products, body(): jnp.einsum('sqb,jsiqw->jibw', own_onehot, chosen, preferred_element_type=...  20.6 us
    select_n x1, other arithmetic, pick_rows(): jnp.where(present[:, :, None, None, None], chosen, jnp.zeros((), chosen.d...  7.19 us
    gather x1, local copies, waits for them, and re-layouts, pick_rows(): chosen = products[supernode_ids, position]  6.87 us
    dot_general x1, matrix products, body(): jnp.einsum('spiw,sqmw->spiqm', own_solved, lax.all_gather(own_solved, 'ro...  6.66 us
  transfers between devices with their start and end apart: 2, of which 2 were waited for; matrix products, arithmetic and copies ran while one was open for 1% of the time, Pallas kernels for 0%

commit v1 on v0

--- a/solution.py
+++ b/solution.py
@@ -2,6 +2,19 @@
 import jax.numpy as jnp
 from jax import lax
 from jax.sharding import PartitionSpec as P
+
+
+def gather_around(x, axis, dim):
+    ways = lax.axis_size(axis)
+    up = [(d, (d + 1) % ways) for d in range(ways)]
+    down = [(d, (d - 1) % ways) for d in range(ways)]
+    earlier, later = ([x], [x])
+    for _ in range(ways // 2):
+        earlier.append(lax.ppermute(earlier[-1], axis, up))
+    for _ in range((ways - 1) // 2):
+        later.append(lax.ppermute(later[-1], axis, down))
+    line = jnp.concatenate([*earlier[::-1], *later[1:]], axis=dim)
+    return jnp.roll(line, (lax.axis_index(axis) - ways // 2) * x.shape[dim], axis=dim)
 
 
 def solve_rows(blocks, factor_inverse):
@@ -31,7 +44,7 @@
     products = jnp.einsum(
         "spiw,sqmw->spiqm",
         own_solved,
-        lax.all_gather(own_solved, "row", axis=2, tiled=True),
+        gather_around(own_solved, "row", 2),
         preferred_element_type=jnp.float32,
     ).astype(jnp.bfloat16)
     block_ids = lax.broadcasted_iota(jnp.int32, (1, 1, 1, ancestors), 3)

time: 329 us -> 335 us (1.018)
  starting transfers between devices: 0.04 us -> 14.3 us
  waiting for transfers between devices: 228 us -> 221 us
    all_gather x1 -> x0, waiting for transfers between devices: 33.7 us -> none  [body(): lax.all_gather(own_solved, 'row', axis=2, tiled=True)]
    ppermute x0 -> x7, waiting for transfers between devices: none -> 21.7 us  [the longest x4 17.1 us: gather_around(): earlier.append(lax.ppermute(earlier[-1], axis, up))]
    ppermute x0 -> x7, starting transfers between devices: none -> 14.3 us  [the longest x4 10.5 us: gather_around(): earlier.append(lax.ppermute(earlier[-1], axis, up))]
    unnamed x3 -> x2, waiting for transfers between devices: 194 us -> 199 us
  transfers between devices with their start and end apart: 2 -> 8, of which waited for: 2 -> 7; matrix products, arithmetic and copies ran while one was open for 1% -> 1% of each run, Pallas kernels for 0% -> 0%
where the time goes in v1:
time: 335 us; the launch traced here: 334 us
  waiting for transfers between devices  221 us (66%)
  local copies, waits for them, and re-layouts  47.3 us (14%)
  matrix products  26.6 us (8%)
  starting transfers between devices  14.3 us (4%)
  between operations  13.5 us (4%)
  other arithmetic  11.8 us (4%)
    unnamed x2, waiting for transfers between devices  199 us
    reshape x1, local copies, waits for them, and re-layouts, body(): spread.reshape(ancestor_rows.shape[0] * lax.axis_size('col'), own_height,...  35.9 us
    dot_general x1, matrix products, body(): jnp.einsum('sqb,jsiqw->jibw', own_onehot, chosen, preferred_element_type=...  20.6 us
    ppermute x4, waiting for transfers between devices, gather_around(): earlier.append(lax.ppermute(earlier[-1], axis, up))  17.1 us
    ppermute x4, starting transfers between devices, gather_around(): earlier.append(lax.ppermute(earlier[-1], axis, up))  10.5 us
    select_n x1, other arithmetic, pick_rows(): jnp.where(present[:, :, None, None, None], chosen, jnp.zeros((), chosen.d...  7.2 us
    gather x1, local copies, waits for them, and re-layouts, pick_rows(): chosen = products[supernode_ids, position]  6.87 us
  transfers between devices with their start and end apart: 8, of which 7 were waited for; matrix products, arithmetic and copies ran while one was open for 1% of the time, Pallas kernels for 0%

profile of v1, /device:TPU:1, one launch (start us, length us, event | category | flops | bytes accessed | tf_op | source)
XLA Modules:
  0.0 334.1 jit_solution(1745991704207586773)
XLA Ops:
  6.5 1.0 copy-done
  7.6 1.5 convolution_convert_fusion
  9.1 3.0 collective-permute-start
  12.1 6.1 %collective-permute-done = bf16[1,8,64,512]{3,2,1,0:T(8,128)(2,1)S(1)} collective-permute-done((bf16[1,8,64,512]{3,2,1,0:T(8,128)(2,1)S(1)}, bf16[1,8,64,512]{3,2,1,0:T(8,128)(2,1)S(1)}, u32[]{:S(2)}, u32[]{:S(2)}) %collective-permute-start) | collective-permute-done | bytes 524320 | tf_op jit(solution)/shard_map/ppermute | solution.py:13
  18.3 2.5 collective-permute-start.1
  21.0 5.9 %collective-permute-done.1 = bf16[1,8,64,512]{3,2,1,0:T(8,128)(2,1)S(1)} collective-permute-done((bf16[1,8,64,512]{3,2,1,0:T(8,128)(2,1)S(1)}, bf16[1,8,64,512]{3,2,1,0:T(8,128)(2,1)S(1)}, u32[]{:S(2)}, u32[]{:S(2)}) %collective-permute-start.1) | collective-permute-done | bytes 524320 | tf_op jit(solution)/shard_map/ppermute | solution.py:13
  26.9 2.5 collective-permute-start.2
  29.3 0.9 dynamic-slice_reduce_fusion
  31.0 1.4 collective-permute-start.5
  32.4 3.1 collective-permute-done.2
  35.5 2.5 collective-permute-start.3
  38.7 1.2 collective-permute-done.5
  39.9 2.2 collective-permute-start.6
  42.0 2.0 collective-permute-done.3
  44.1 1.1 constant_dynamic-update-slice_fusion.15
  45.4 3.5 %collective-permute-done.6 = bf16[1,8,64,512]{3,2,1,0:T(8,128)(2,1)S(1)} collective-permute-done((bf16[1,8,64,512]{3,2,1,0:T(8,128)(2,1)S(1)}, bf16[1,8,64,512]{3,2,1,0:T(8,128)(2,1)S(1)}, u32[]{:S(2)}, u32[]{:S(2)}) %collective-permute-start.6) | collective-permute-done | bytes 524320 | tf_op jit(solution)/shard_map/ppermute | solution.py:15
  48.9 1.1 constant_dynamic-update-slice_fusion.7
  50.3 4.4 %convert_bitcast_fusion = bf16[1,8,64,8,512]{4,2,3,1,0:T(8,128)(2,1)} fusion(bf16[1,8,1024,512]{3,2,1,0:T(8,128)(2,1)S(1)} %constant_dynamic-update-slice_fusion, s32[]{:T(128)S(6)} %select_n.64, bf16[8,64,512]{2,1,0:T(8,128)(2,1)S(1)} %convolution_convert_fusion), kind=kOutput, calls=%fused_computation.7 | convolution fusion | flops 2149580800 | bytes 8912900 | tf_op jit(solution)/shard_map/spiw,sqmw->spiqm/dot_general | solution.py:44
  54.8 6.9 %gather_fusion = bf16[16,64,8,512]{3,1,2,0:T(8,128)(2,1)} fusion(bf16[1,8,64,8,512]{4,2,3,1,0:T(8,128)(2,1)} %convert_bitcast_fusion, s32[16]{0:T(128)S(1)} %or_bitcast_fusion), kind=kCustom, calls=%fused_computation | custom fusion | bytes 16777344 | tf_op jit(solution)/shard_map/gather | solution.py:32
  61.6 7.2 %fusion = bf16[16,64,8,512]{3,1,2,0:T(8,128)(2,1)} fusion(bf16[16,64,8,512]{3,1,2,0:T(8,128)(2,1)} %gather_fusion, pred[16]{0:T(512)(128)(4,1)S(1)} %compare_reduce_fusion), kind=kLoop, calls=%fused_computation.3 | loop fusion | flops 4194304 | bytes 16777232 | tf_op jit(solution)/shard_map/jit(_where)/select_n | solution.py:33
  68.8 20.6 %convolution_bitcast_fusion = f32[16,64,16,512]{3,2,1,0:T(8,128)} fusion(bf16[16,64,8,512]{3,1,2,0:T(8,128)(2,1)} %fusion, s32[8]{0:T(128)S(1)} %dynamic-slice_reduce_fusion), kind=kOutput, calls=%fused_computation.1 | convolution fusion | flops 134217856 | bytes 41943072 | tf_op jit(solution)/shard_map/sqb,jsiqw->jibw/dot_general | solution.py:53
  89.5 35.9 %reshape.219 = f32[16,64,8192]{2,1,0:T(8,128)} reshape(f32[16,64,16,512]{3,2,1,0:T(8,128)} %convolution_bitcast_fusion) | data formatting | bytes 67108864 | tf_op jit(solution)/shard_map/reshape | solution.py:55
  125.4 198.8 %reduce-scatter.4.cloned.1.call-done = f32[1,64,8192]{2,1,0:T(8,128)} async-done(((f32[16,64,8192]{2,1,0:T(8,128)}), f32[1,64,8192]{2,1,0:T(8,128)}) %reduce-scatter.4.cloned.1.call-update) | async-done | bytes 2097168
  324.1 3.1 sub.12
  (28 shorter events, 2.3 us)
Async XLA Ops:
  6.5 1.0 copy-start
  6.5 317.6 %reduce-scatter.4.cloned.1.call-start = ((), (), s32[]{:S(2)}) async-start(), calls=%async_computation.1 | async-start | bytes 35651584
  9.1 9.2 %collective-permute-start = (bf16[1,8,64,512]{3,2,1,0:T(8,128)(2,1)S(1)}, bf16[1,8,64,512]{3,2,1,0:T(8,128)(2,1)S(1)}, u32[]{:S(2)}, u32[]{:S(2)}) collective-permute-start(bf16[1,8,64,512]{3,2,1,0:T(8,128)(2,1)S(1)} %bitcast.47), channel_id=1, source_target_pairs={{0,16},{16,32},{32,48},{48,64},{64,80},{80,96},{96,112},{112,0},{1... | collective-permute-start | bytes 1572872 | tf_op jit(solution)/shard_map/ppermute | solution.py:13
  18.3 8.6 %collective-permute-start.1 = (bf16[1,8,64,512]{3,2,1,0:T(8,128)(2,1)S(1)}, bf16[1,8,64,512]{3,2,1,0:T(8,128)(2,1)S(1)}, u32[]{:S(2)}, u32[]{:S(2)}) collective-permute-start(bf16[1,8,64,512]{3,2,1,0:T(8,128)(2,1)S(1)} %collective-permute-done), channel_id=1, source_target_pairs={{0,16},{16,32},{32,48},{48,64},{64,80},{80,96},{96,112},{112,0},{1... | collective-permute-start | bytes 1572872 | tf_op jit(solution)/shard_map/ppermute | solution.py:13
  20.7 10.2 %collective-permute-start.4 = (bf16[1,8,64,512]{3,2,1,0:T(8,128)(2,1)S(1)}, bf16[1,8,64,512]{3,2,1,0:T(8,128)(2,1)S(1)}, u32[]{:S(2)}, u32[]{:S(2)}) collective-permute-start(bf16[1,8,64,512]{3,2,1,0:T(8,128)(2,1)S(1)} %bitcast.48), channel_id=1, source_target_pairs={{0,112},{16,0},{32,16},{48,32},{64,48},{80,64},{96,80},{112,96},{1... | collective-permute-start | bytes 1572872 | tf_op jit(solution)/shard_map/ppermute | solution.py:15
  26.9 8.6 %collective-permute-start.2 = (bf16[1,8,64,512]{3,2,1,0:T(8,128)(2,1)S(1)}, bf16[1,8,64,512]{3,2,1,0:T(8,128)(2,1)S(1)}, u32[]{:S(2)}, u32[]{:S(2)}) collective-permute-start(bf16[1,8,64,512]{3,2,1,0:T(8,128)(2,1)S(1)} %collective-permute-done.1), channel_id=1, source_target_pairs={{0,16},{16,32},{32,48},{48,64},{64,80},{80,96},{96,112},{112,0},{1... | collective-permute-start | bytes 1572872 | tf_op jit(solution)/shard_map/ppermute | solution.py:13
  31.0 8.9 %collective-permute-start.5 = (bf16[1,8,64,512]{3,2,1,0:T(8,128)(2,1)S(1)}, bf16[1,8,64,512]{3,2,1,0:T(8,128)(2,1)S(1)}, u32[]{:S(2)}, u32[]{:S(2)}) collective-permute-start(bf16[1,8,64,512]{3,2,1,0:T(8,128)(2,1)S(1)} %collective-permute-done.4), channel_id=1, source_target_pairs={{0,112},{16,0},{32,16},{48,32},{64,48},{80,64},{96,80},{112,96},{1... | collective-permute-start | bytes 1572872 | tf_op jit(solution)/shard_map/ppermute | solution.py:15
  35.5 8.6 %collective-permute-start.3 = (bf16[1,8,64,512]{3,2,1,0:T(8,128)(2,1)S(1)}, bf16[1,8,64,512]{3,2,1,0:T(8,128)(2,1)}, u32[]{:S(2)}, u32[]{:S(2)}) collective-permute-start(bf16[1,8,64,512]{3,2,1,0:T(8,128)(2,1)S(1)} %collective-permute-done.2), channel_id=1, source_target_pairs={{0,16},{16,32},{32,48},{48,64},{64,80},{80,96},{96,112},{112,0},{1... | collective-permute-start | bytes 1572872 | tf_op jit(solution)/shard_map/ppermute | solution.py:13
  39.9 9.0 %collective-permute-start.6 = (bf16[1,8,64,512]{3,2,1,0:T(8,128)(2,1)S(1)}, bf16[1,8,64,512]{3,2,1,0:T(8,128)(2,1)S(1)}, u32[]{:S(2)}, u32[]{:S(2)}) collective-permute-start(bf16[1,8,64,512]{3,2,1,0:T(8,128)(2,1)S(1)} %collective-permute-done.5), channel_id=1, source_target_pairs={{0,112},{16,0},{32,16},{48,32},{64,48},{80,64},{96,80},{112,96},{1... | collective-permute-start | bytes 1572872 | tf_op jit(solution)/shard_map/ppermute | solution.py:15
  125.3 198.8 %copy-start.2 = (f32[1,64,8192]{2,1,0:T(8,128)S(1)}, f32[1,64,8192]{2,1,0:T(8,128)}, u32[]{:S(2)}) copy-start(f32[1,64,8192]{2,1,0:T(8,128)} %param.9) | copy-start | bytes 6291460
  125.4 201.9 %copy-start.1 = (bf16[1,512,512]{2,1,0:T(8,128)(2,1)S(1)}, bf16[1,512,512]{2,1,0:T(8,128)(2,1)}, u32[]{:S(2)}) copy-start(bf16[1,512,512]{2,1,0:T(8,128)(2,1)} %param.6) | copy-start | bytes 1572868
Sparse Core Ops, SparseCore 0:
  125.5 198.6 reduce-scatter.3
